TPU v7x, 32 devices: a whole 2x2x4 slice. The times are simulated.
32 devices in a mesh: wide: 8 (over z, y), narrow: 4 (over x, core).
Axes of the slice: x: 2, y: 2, z: 4, core: 2. Of those that a mesh axis runs over, the one named last changes fastest.
Arguments:
- entry_factor: bfloat16 [288, 4, 64, 1024], P('wide', 'narrow'), may hold values from -6 to 6
- entry_panel: int32 [288, 4], P('wide', 'narrow'), may hold values from 0 to 1
- entry_target: int32 [288, 4], P('wide', 'narrow'), may hold values from 0 to 7, as said below
- entry_count: int32 [4, 8], P('narrow', 'wide'), may hold values from 1 to 36, 96 in all within a row
- panel_shared: bfloat16 [16, 64, 1024], P('wide', None, 'narrow'), may hold values from -0.1875 to 0.1875
- coupling: float32 [16, 64, 64], P('wide'), may hold values from -0.75 to 0.75
- probes: bfloat16 [32, 64, 1024], P('narrow'), may hold values from -6 to 6
Outputs:
- left_factor: float32 [32, 64, 1024], P('narrow', None, 'wide')
- right_factor: float32 [32, 64, 1024], P('narrow', None, 'wide')
Inputs may be any that keep to these rules, and one draw needn't show every extreme that they name: `entry_panel`: the local panel of an entry of any slot, live or not. `entry_target`: the local target of an entry; every target has at least one live entry. `entry_count`: the live slots of one device; for every owner the counts over the 8 wide indices sum to 96, and some device holds exactly 36.
All inputs are finite; a program needn't handle non-finite values.
Results may differ from a plain program's by a relative error of at most 0.0036.
Values may be sent and summed in bfloat16 or wider, within the bound.
A program may use at most 64 MiB of HBM per device.

v0:
```python
import math
import jax
import jax.numpy as jnp
from jax import lax
from jax.sharding import PartitionSpec as P


def wide_reduce(x, count):
    lead, rows, width = x.shape
    pieces = x.reshape(lead, rows, count, width // count).transpose(2, 0, 1, 3)
    pieces = lax.all_to_all(pieces, "wide", 0, 0, tiled=True)
    return pieces.sum(axis=0)


def wide_gather(x, count):
    lead, rows, width = x.shape
    copies = jnp.broadcast_to(x[None], (count, lead, rows, width))
    copies = lax.all_to_all(copies, "wide", 0, 0, tiled=True)
    return copies.transpose(1, 2, 0, 3).reshape(lead, rows, count * width)


def lower_inverse(lower):
    highest = lax.Precision.HIGHEST
    size = lower.shape[-1]
    eye = jnp.eye(size, dtype=lower.dtype)
    diag = jnp.diagonal(lower, axis1=-2, axis2=-1)
    strict = eye - lower / diag[..., :, None]
    unit_inverse = eye + strict
    power = strict
    for _ in range(max(size - 1, 1).bit_length() - 1):
        power = jnp.einsum("tij,tjk->tik", power, power, precision=highest)
        unit_inverse = unit_inverse + jnp.einsum(
            "tij,tjk->tik", unit_inverse, power, precision=highest
        )
    return unit_inverse / diag[..., None, :]


def shards(entry_factor, entry_panel, entry_target, entry_count, panel_shared, coupling, probes):
    highest = lax.Precision.HIGHEST
    factors = entry_factor[:, 0]
    slot_count = factors.shape[0]
    rank_dim = factors.shape[1]
    full_width = factors.shape[2]
    panel_count = panel_shared.shape[0]
    target_count = probes.shape[0]
    live_mask = (jnp.arange(slot_count) < entry_count[0, 0]).astype(jnp.float32)
    pick_panel = (entry_panel == jnp.arange(panel_count)[None, :]).astype(jnp.float32) * live_mask[
        :, None
    ]
    pick_target = (entry_target == jnp.arange(target_count)[None, :]).astype(jnp.float32)
    pair_pick = (pick_panel[:, :, None] * pick_target[:, None, :]).reshape(
        slot_count, panel_count * target_count
    )
    gathered = lax.all_gather(panel_shared, "narrow", axis=2, tiled=True)
    projected = jnp.einsum("drb,tkb->dtrk", gathered, probes, preferred_element_type=jnp.float32)
    coefficients = jnp.einsum("dij,dtjk->dtik", coupling, projected, precision=highest).astype(
        jnp.bfloat16
    )
    coeff_table = coefficients.reshape(panel_count * target_count, rank_dim * rank_dim)
    chosen = jnp.dot(
        pair_pick.astype(jnp.bfloat16), coeff_table, preferred_element_type=jnp.float32
    )
    chosen = chosen.astype(jnp.bfloat16).reshape(slot_count, rank_dim, rank_dim)
    contributions = jnp.einsum("eji,ejb->eib", chosen, factors, preferred_element_type=jnp.float32)
    sketch = jnp.einsum("et,eib->tib", pick_target, contributions, precision=highest)
    wide_count = lax.axis_size("wide")
    share_cols = full_width // wide_count
    sketch_own = wide_reduce(sketch, wide_count)
    gram_part = jnp.einsum("tib,tjb->tij", sketch_own, sketch_own, precision=highest)
    gram_copies = jnp.broadcast_to(gram_part[None], (wide_count,) + gram_part.shape)
    gram_matrix = lax.all_to_all(gram_copies, "wide", 0, 0, tiled=True).sum(axis=0)
    sketch_sum = wide_gather(sketch_own, wide_count)
    lower_factor = jnp.linalg.cholesky(gram_matrix)
    basis = jnp.einsum("tij,tjb->tib", lower_inverse(lower_factor), sketch_sum, precision=highest)
    basis_round = basis.astype(jnp.bfloat16)
    own_basis = lax.dynamic_slice_in_dim(basis, lax.axis_index("wide") * share_cols, share_cols, 2)
    selected = jnp.einsum(
        "et,tkb->ekb",
        pick_target.astype(jnp.bfloat16),
        basis_round,
        preferred_element_type=jnp.float32,
    )
    selected = selected.astype(jnp.bfloat16)
    back_terms = jnp.einsum("eib,ekb->eik", factors, selected, preferred_element_type=jnp.float32)
    summed = jnp.einsum("ep,eik->pik", pair_pick, back_terms, precision=highest)
    summed = summed.reshape(panel_count, target_count, rank_dim, rank_dim)
    middle_terms = jnp.einsum("dtik,dij->dtkj", summed, coupling, precision=highest)
    partial_rows = jnp.einsum(
        "dtkj,djb->tkb", middle_terms, gathered.astype(jnp.float32), precision=highest
    )
    coeff_part = wide_reduce(partial_rows, wide_count)
    root_width = math.sqrt(full_width)
    return (own_basis * root_width, coeff_part / root_width)


def solution(mesh):
    placed = (
        P("wide", "narrow", None, None),
        P("wide", "narrow"),
        P("wide", "narrow"),
        P("narrow", "wide"),
        P("wide", None, "narrow"),
        P("wide", None, None),
        P("narrow", None, None),
    )
    return jax.shard_map(
        shards,
        mesh=mesh,
        in_specs=placed,
        out_specs=(P("narrow", None, "wide"), P("narrow", None, "wide")),
        check_vma=False,
    )
```

profile of v0, /device:TPU:0, one launch (start us, length us, event | category | flops | bytes accessed | tf_op | source)
XLA Modules:
  0.0 250.5 jit_solution(6765023599289800090)
XLA Ops:
  0.7 0.7 fusion.42
  1.4 7.4 %all_gather.3 = bf16[2,64,1024]{2,1,0:T(8,128)(2,1)S(1)} all-gather(bf16[2,64,256]{2,1,0:T(8,128)(2,1)} %param.11), channel_id=1, replica_groups=mesh['wide'=8,'narrow'=4] {'narrow'}, dimensions={2}, use_global_device_ids=true | all-gather | bytes 327680 | tf_op jit(solution)/shard_map/all_gather | solution.py:54
  12.2 3.8 %fusion.4 = f32[36,64,1024]{2,1,0:T(8,128)S(1)} fusion(bf16[36,64,64]{2,1,0:T(8,128)(2,1)S(1)} %reshape.114, bf16[36,1,64,1024]{3,2,1,0:T(8,128)(2,1)} %param.7), kind=kOutput, calls=%fused_computation.5 | convolution fusion | flops 301989888 | bytes 14450688 | tf_op jit(solution)/shard_map/eji,ejb->eib/dot_general | solution.py:64
  16.0 8.9 %fusion.10 = f32[8,64,8,128]{3,0,2,1:T(8,128)S(1)} fusion(f32[36,64,1024]{2,1,0:T(8,128)S(1)} %fusion.4, s32[36]{0:T(128)S(1)} %bitcast.117), kind=kOutput, calls=%fused_computation.15 | convolution fusion | flops 226492704 | bytes 11534480 | tf_op jit(solution)/shard_map/et,eib->tib/dot_general | solution.py:65
  25.0 54.4 %all_to_all.20 = f32[8,8,64,128]{3,1,2,0:T(8,128)S(1)} all-to-all(f32[8,8,64,128]{3,1,2,0:T(8,128)S(1)} %bitcast.114), channel_id=1, replica_groups=mesh['wide'=8,'narrow'=4] {'wide'}, dimensions={0} | all-to-all | bytes 4194304 | tf_op jit(solution)/shard_map/all_to_all | solution.py:11
  80.3 2.1 reshape.132
  82.5 3.6 %all-to-all-start.1 = ((f32[8,1,32768]{2,1,0:T(1,128)}), f32[8,1,32768]{2,1,0:T(1,128)S(1)}, u32[]{:S(2)}, u32[]{:S(2)}) async-start(f32[8,1,32768]{2,1,0:T(1,128)} %reshape.132), calls=%async_computation.1 | async-start | bytes 2097152 | tf_op jit(solution)/shard_map/all_to_all | solution.py:71
  86.2 25.8 %all-to-all-done.1 = f32[8,1,32768]{2,1,0:T(1,128)S(1)} async-done(((f32[8,1,32768]{2,1,0:T(1,128)}), f32[8,1,32768]{2,1,0:T(1,128)S(1)}, u32[]{:S(2)}, u32[]{:S(2)}) %all-to-all-start.1) | async-done | bytes 1048608 | tf_op jit(solution)/shard_map/all_to_all | solution.py:71
  112.0 1.6 broadcast_in_dim.12
  113.5 4.3 %all-to-all-start.2 = ((f32[8,8,64,128]{3,2,1,0:T(8,128)}), f32[8,8,64,128]{3,2,1,0:T(8,128)}, u32[]{:S(2)}, u32[]{:S(2)}) async-start(f32[8,8,64,128]{3,2,1,0:T(8,128)} %broadcast_in_dim.12), calls=%async_computation.2 | async-start | bytes 4194304 | tf_op jit(solution)/shard_map/all_to_all | solution.py:18
  118.4 4.5 %reduce.6 = f32[8,32768]{1,0:T(8,128)} reduce(f32[8,1,32768]{2,1,0:T(1,128)S(1)} %all-to-all-done.1, f32[]{:T(128)} %broadcast.125), dimensions={1}, to_apply=%all_to_all.13.reduce_sub_computation | reduce | bytes 2097156 | tf_op jit(solution)/shard_map/all_to_all | solution.py:71
  122.9 2.1 reshape.133
  125.4 47.1 %custom-call.4 = f32[8,64,64]{2,1,0:T(8,128)S(1)} custom-call(f32[8,64,64]{2,1,0:T(8,128)S(1)} %fusion.27), custom_call_target="Cholesky" | custom-call | tf_op jit(solution)/shard_map/jit(cholesky)/cholesky | solution.py:73
  173.4 0.9 gather_fusion
  178.6 4.7 %fusion.50 = (bf16[8,64,1024]{2,1,0:T(8,128)(2,1)S(1)}, f32[8,64,1024]{2,1,0:T(8,128)}) fusion(f32[8,64,64]{2,1,0:T(8,128)S(1)} %fusion.21, f32[8,8,64,128]{3,2,1,0:T(8,128)} %all-to-all-done.2), kind=kOutput, calls=%fused_computation.69 | convolution fusion | flops 403177472 | bytes 5373952 | tf_op jit(solution)/shard_map/tij,tjb->tib/dot_general | solution.py:74
  183.3 1.6 convolution_convert_fusion.1
  184.9 5.5 %fusion.13 = f32[36,64,64]{1,2,0:T(8,128)S(1)} fusion(bf16[36,1,64,1024]{3,2,1,0:T(8,128)(2,1)} %param.7, bf16[36,64,1024]{2,0,1:T(8,128)(2,1)S(1)} %convolution_convert_fusion.1), kind=kOutput, calls=%fused_computation.17 | convolution fusion | flops 301989888 | bytes 10027008 | tf_op jit(solution)/shard_map/eib,ekb->eik/dot_general | solution.py:84
  190.9 1.0 fusion.18
  191.9 1.8 fusion.24
  193.8 1.0 convolution_bitcast_fusion
  194.8 1.6 copy.85
  196.4 5.9 %all-to-all-start.3 = ((f32[8,8,64,128]{3,2,1,0:T(8,128)}), f32[8,8,64,128]{3,2,1,0:T(8,128)S(1)}, u32[]{:S(2)}, u32[]{:S(2)}) async-start(f32[8,8,64,128]{3,2,1,0:T(8,128)} %bitcast.113), calls=%async_computation.3 | async-start | bytes 4194304 | tf_op jit(solution)/shard_map/all_to_all | solution.py:11
  202.4 1.7 dynamic-slice_multiply_fusion
  204.0 45.6 %all-to-all-done.3 = f32[8,8,64,128]{3,2,1,0:T(8,128)S(1)} async-done(((f32[8,8,64,128]{3,2,1,0:T(8,128)}), f32[8,8,64,128]{3,2,1,0:T(8,128)S(1)}, u32[]{:S(2)}, u32[]{:S(2)}) %all-to-all-start.3) | async-done | bytes 2097184 | tf_op jit(solution)/shard_map/all_to_all | solution.py:11
  (52 shorter events, 11.1 us)
Async XLA Ops:
  0.6 8.2 %copy-start = (bf16[8,64,1024]{2,1,0:T(8,128)(2,1)S(1)}, bf16[8,64,1024]{2,1,0:T(8,128)(2,1)}, u32[]{:S(2)}) copy-start(bf16[8,64,1024]{2,1,0:T(8,128)(2,1)} %param.13) | copy-start | bytes 3145732
  0.6 8.9 %copy-start.3 = (f32[2,64,64]{2,1,0:T(8,128)S(1)}, f32[2,64,64]{2,1,0:T(8,128)}, u32[]{:S(2)}) copy-start(f32[2,64,64]{2,1,0:T(8,128)} %param.12) | copy-start | bytes 98308
  0.7 10.6 %copy-start.5 = (s32[36,1]{0,1:T(1,128)S(1)}, s32[36,1]{0,1:T(1,128)}, u32[]{:S(2)}) copy-start(s32[36,1]{0,1:T(1,128)} %param.8) | copy-start | bytes 436
  8.8 0.7 copy-start.1
  12.2 3.8 %copy-start.4 = (s32[36,1]{0,1:T(1,128)S(1)}, s32[36,1]{0,1:T(1,128)}, u32[]{:S(2)}) copy-start(s32[36,1]{0,1:T(1,128)} %param.9) | copy-start | bytes 436
  82.5 29.5 %all-to-all-start.1 = ((f32[8,1,32768]{2,1,0:T(1,128)}), f32[8,1,32768]{2,1,0:T(1,128)S(1)}, u32[]{:S(2)}, u32[]{:S(2)}) async-start(f32[8,1,32768]{2,1,0:T(1,128)} %reshape.132), calls=%async_computation.1 | async-start | bytes 2097152 | tf_op jit(solution)/shard_map/all_to_all | solution.py:71
  113.5 65.1 %all-to-all-start.2 = ((f32[8,8,64,128]{3,2,1,0:T(8,128)}), f32[8,8,64,128]{3,2,1,0:T(8,128)}, u32[]{:S(2)}, u32[]{:S(2)}) async-start(f32[8,8,64,128]{3,2,1,0:T(8,128)} %broadcast_in_dim.12), calls=%async_computation.2 | async-start | bytes 4194304 | tf_op jit(solution)/shard_map/all_to_all | solution.py:18
  190.9 2.9 %copy-start.2 = (bf16[2,64,1024]{2,1,0:T(8,128)(2,1)S(1)}, bf16[2,64,1024]{2,1,0:T(8,128)(2,1)}, u32[]{:S(2)}) copy-start(bf16[2,64,1024]{2,1,0:T(8,128)(2,1)} %copy-done.1) | copy-start | bytes 786436
  196.4 53.1 %all-to-all-start.3 = ((f32[8,8,64,128]{3,2,1,0:T(8,128)}), f32[8,8,64,128]{3,2,1,0:T(8,128)S(1)}, u32[]{:S(2)}, u32[]{:S(2)}) async-start(f32[8,8,64,128]{3,2,1,0:T(8,128)} %bitcast.113), calls=%async_computation.3 | async-start | bytes 4194304 | tf_op jit(solution)/shard_map/all_to_all | solution.py:11
where the time goes:
time: 251 us; the launch traced here: 250 us
  waiting for transfers between devices  71.4 us (28%)
  blocking collectives  61.8 us (25%)
  other arithmetic  55.6 us (22%)
  matrix products  34.3 us (14%)
  starting transfers between devices  13.9 us (6%)
  local copies, waits for them, and re-layouts  11.9 us (5%)
    all_to_all x1, blocking collectives, wide_reduce(): pieces = lax.all_to_all(pieces, 'wide', 0, 0, tiled=True)  54.4 us
    another operation x3, other arithmetic, shards(): lower_factor = jnp.linalg.cholesky(gram_matrix)  47.3 us
    all_to_all x1, waiting for transfers between devices, wide_reduce(): pieces = lax.all_to_all(pieces, 'wide', 0, 0, tiled=True)  45.6 us
    all_to_all x1, waiting for transfers between devices, shards(): lax.all_to_all(gram_copies, 'wide', 0, 0, tiled=True).sum(axis=0)  25.8 us
    dot_general x1, matrix products, shards(): jnp.einsum('et,eib->tib', pick_target, contributions, precision=highest)  8.9 us
    all_gather x1, blocking collectives, shards(): gathered = lax.all_gather(panel_shared, 'narrow', axis=2, tiled=True)  7.42 us
    all_to_all x1, starting transfers between devices, wide_reduce(): pieces = lax.all_to_all(pieces, 'wide', 0, 0, tiled=True)  5.91 us
    dot_general x1, matrix products, shards(): jnp.einsum('eib,ekb->eik', factors, selected, preferred_element_type=jnp....  5.48 us
  transfers between devices with their start and end apart: 3, of which 2 were waited for; matrix products, arithmetic and copies ran while one was open for 25% of the time, Pallas kernels for 0%

commit v1 on v0

--- a/solution.py
+++ b/solution.py
@@ -3,6 +3,18 @@
 import jax.numpy as jnp
 from jax import lax
 from jax.sharding import PartitionSpec as P
+
+
+def doubled_up(x, axis, dim):
+    ways, here, step = (lax.axis_size(axis), lax.axis_index(axis), x.shape[dim])
+    line, have = (x, 1)
+    while have < ways:
+        line = jnp.concatenate(
+            [line, lax.ppermute(line, axis, [(d, (d - have) % ways) for d in range(ways)])],
+            axis=dim,
+        )
+        have = 2 * have
+    return jnp.roll(line, here * step, axis=dim)
 
 
 def wide_reduce(x, count):
@@ -51,7 +63,7 @@
     pair_pick = (pick_panel[:, :, None] * pick_target[:, None, :]).reshape(
         slot_count, panel_count * target_count
     )
-    gathered = lax.all_gather(panel_shared, "narrow", axis=2, tiled=True)
+    gathered = doubled_up(panel_shared, "narrow", 2)
     projected = jnp.einsum("drb,tkb->dtrk", gathered, probes, preferred_element_type=jnp.float32)
     coefficients = jnp.einsum("dij,dtjk->dtik", coupling, projected, precision=highest).astype(
         jnp.bfloat16

time: 251 us -> 255 us (1.016)
  blocking collectives: 61.8 us -> 53.8 us
  waiting for transfers between devices: 71.4 us -> 75.7 us
  starting transfers between devices: 13.9 us -> 16.9 us
    all_gather x1 -> x0, blocking collectives: 7.42 us -> none  [shards(): gathered = lax.all_gather(panel_shared, 'narrow', axis=2, tiled=True)]
    ppermute x0 -> x2, waiting for transfers between devices: none -> 4.84 us  [doubled_up(): lax.ppermute(line, axis, [(d, (d - have) % ways) for d in range(ways)])]
    ppermute x0 -> x2, starting transfers between devices: none -> 3.09 us  [doubled_up(): lax.ppermute(line, axis, [(d, (d - have) % ways) for d in range(ways)])]
    unnamed x14 -> x17, local copies, waits for them, and re-layouts: 4.46 us -> 6.74 us
  transfers between devices with their start and end apart: 3 -> 5, of which waited for: 2 -> 4; matrix products, arithmetic and copies ran while one was open for 25% -> 25% of each run, Pallas kernels for 0% -> 0%
where the time goes in v1:
time: 255 us; the launch traced here: 254 us
  waiting for transfers between devices  75.7 us (30%)
  other arithmetic  57 us (22%)
  blocking collectives  53.8 us (21%)
  matrix products  35 us (14%)
  starting transfers between devices  16.9 us (7%)
  local copies, waits for them, and re-layouts  14.1 us (6%)
    all_to_all x1, blocking collectives, wide_reduce(): pieces = lax.all_to_all(pieces, 'wide', 0, 0, tiled=True)  53.8 us
    another operation x3, other arithmetic, shards(): lower_factor = jnp.linalg.cholesky(gram_matrix)  47.3 us
    all_to_all x1, waiting for transfers between devices, wide_reduce(): pieces = lax.all_to_all(pieces, 'wide', 0, 0, tiled=True)  45.4 us
    all_to_all x1, waiting for transfers between devices, shards(): lax.all_to_all(gram_copies, 'wide', 0, 0, tiled=True).sum(axis=0)  25.5 us
    dot_general x1, matrix products, shards(): jnp.einsum('et,eib->tib', pick_target, contributions, precision=highest)  8.9 us
    unnamed x17, local copies, waits for them, and re-layouts  6.74 us
    all_to_all x1, starting transfers between devices, wide_reduce(): pieces = lax.all_to_all(pieces, 'wide', 0, 0, tiled=True)  5.9 us
    dot_general x1, matrix products, shards(): jnp.einsum('eib,ekb->eik', factors, selected, preferred_element_type=jnp....  5.48 us
  transfers between devices with their start and end apart: 5, of which 4 were waited for; matrix products, arithmetic and copies ran while one was open for 25% of the time, Pallas kernels for 0%

profile of v1, /device:TPU:0, one launch (start us, length us, event | category | flops | bytes accessed | tf_op | source)
XLA Modules:
  0.0 254.2 jit_solution(18062857953686306918)
XLA Ops:
  0.7 2.5 collective-permute-start
  7.7 4.6 %collective-permute-done.1 = bf16[2,64,512]{2,1,0:T(8,128)(2,1)S(1)} collective-permute-done((bf16[2,64,512]{2,1,0:T(8,128)(2,1)S(1)}, bf16[2,64,512]{2,1,0:T(8,128)(2,1)S(1)}, u32[]{:S(2)}, u32[]{:S(2)}) %collective-permute-start.1) | collective-permute-done | bytes 131104 | tf_op jit(solution)/shard_map/ppermute | solution.py:13
  14.7 1.0 fusion.20
  17.1 3.8 %fusion.4 = f32[36,64,1024]{2,1,0:T(8,128)S(1)} fusion(bf16[36,64,64]{2,1,0:T(8,128)(2,1)S(1)} %reshape.114, bf16[36,1,64,1024]{3,2,1,0:T(8,128)(2,1)} %param.7), kind=kOutput, calls=%fused_computation.5 | convolution fusion | flops 301989888 | bytes 14450688 | tf_op jit(solution)/shard_map/eji,ejb->eib/dot_general | solution.py:76
  20.8 8.9 %fusion.10 = f32[8,64,8,128]{3,0,2,1:T(8,128)S(1)} fusion(f32[36,64,1024]{2,1,0:T(8,128)S(1)} %fusion.4, s32[36]{0:T(128)S(1)} %bitcast.117), kind=kOutput, calls=%fused_computation.15 | convolution fusion | flops 226492704 | bytes 11534480 | tf_op jit(solution)/shard_map/et,eib->tib/dot_general | solution.py:77
  29.9 53.8 %all_to_all.20 = f32[8,8,64,128]{3,1,2,0:T(8,128)S(1)} all-to-all(f32[8,8,64,128]{3,1,2,0:T(8,128)S(1)} %bitcast.114), channel_id=1, replica_groups=mesh['wide'=8,'narrow'=4] {'wide'}, dimensions={0} | all-to-all | bytes 4194304 | tf_op jit(solution)/shard_map/all_to_all | solution.py:23
  84.6 2.1 reshape.132
  86.7 3.6 %all-to-all-start.1 = ((f32[8,1,32768]{2,1,0:T(1,128)}), f32[8,1,32768]{2,1,0:T(1,128)S(1)}, u32[]{:S(2)}, u32[]{:S(2)}) async-start(f32[8,1,32768]{2,1,0:T(1,128)} %reshape.132), calls=%async_computation.1 | async-start | bytes 2097152 | tf_op jit(solution)/shard_map/all_to_all | solution.py:83
  90.4 25.5 %all-to-all-done.1 = f32[8,1,32768]{2,1,0:T(1,128)S(1)} async-done(((f32[8,1,32768]{2,1,0:T(1,128)}), f32[8,1,32768]{2,1,0:T(1,128)S(1)}, u32[]{:S(2)}, u32[]{:S(2)}) %all-to-all-start.1) | async-done | bytes 1048608 | tf_op jit(solution)/shard_map/all_to_all | solution.py:83
  115.9 1.6 broadcast_in_dim.12
  117.4 4.3 %all-to-all-start.2 = ((f32[8,8,64,128]{3,2,1,0:T(8,128)}), f32[8,8,64,128]{3,2,1,0:T(8,128)}, u32[]{:S(2)}, u32[]{:S(2)}) async-start(f32[8,8,64,128]{3,2,1,0:T(8,128)} %broadcast_in_dim.12), calls=%async_computation.2 | async-start | bytes 4194304 | tf_op jit(solution)/shard_map/all_to_all | solution.py:30
  122.4 4.5 %reduce.6 = f32[8,32768]{1,0:T(8,128)} reduce(f32[8,1,32768]{2,1,0:T(1,128)S(1)} %all-to-all-done.1, f32[]{:T(128)} %broadcast.126), dimensions={1}, to_apply=%all_to_all.13.reduce_sub_computation | reduce | bytes 2097156 | tf_op jit(solution)/shard_map/all_to_all | solution.py:83
  126.9 2.1 reshape.133
  129.3 47.1 %custom-call.4 = f32[8,64,64]{2,1,0:T(8,128)S(1)} custom-call(f32[8,64,64]{2,1,0:T(8,128)S(1)} %fusion.27), custom_call_target="Cholesky" | custom-call | tf_op jit(solution)/shard_map/jit(cholesky)/cholesky | solution.py:85
  182.5 4.7 %fusion.54 = (bf16[8,64,1024]{2,1,0:T(8,128)(2,1)S(1)}, f32[8,64,1024]{2,1,0:T(8,128)}) fusion(f32[8,64,64]{2,1,0:T(8,128)S(1)} %fusion.21, f32[8,8,64,128]{3,2,1,0:T(8,128)} %all-to-all-done.2), kind=kOutput, calls=%fused_computation.80 | convolution fusion | flops 403177472 | bytes 5373952 | tf_op jit(solution)/shard_map/tij,tjb->tib/dot_general | solution.py:86
  187.3 1.6 convolution_convert_fusion.1
  188.8 5.5 %fusion.13 = f32[36,64,64]{1,2,0:T(8,128)S(1)} fusion(bf16[36,1,64,1024]{3,2,1,0:T(8,128)(2,1)} %param.7, bf16[36,64,1024]{2,0,1:T(8,128)(2,1)S(1)} %convolution_convert_fusion.1), kind=kOutput, calls=%fused_computation.17 | convolution fusion | flops 301989888 | bytes 10027008 | tf_op jit(solution)/shard_map/eib,ekb->eik/dot_general | solution.py:96
  194.8 1.0 fusion.18
  195.9 1.8 fusion.24
  197.7 1.0 convolution_bitcast_fusion
  198.7 1.6 copy.88
  200.4 5.9 %all-to-all-start.3 = ((f32[8,8,64,128]{3,2,1,0:T(8,128)}), f32[8,8,64,128]{3,2,1,0:T(8,128)S(1)}, u32[]{:S(2)}, u32[]{:S(2)}) async-start(f32[8,8,64,128]{3,2,1,0:T(8,128)} %bitcast.113), calls=%async_computation.3 | async-start | bytes 4194304 | tf_op jit(solution)/shard_map/all_to_all | solution.py:23
  206.3 1.7 dynamic-slice_multiply_fusion
  208.0 45.4 %all-to-all-done.3 = f32[8,8,64,128]{3,2,1,0:T(8,128)S(1)} async-done(((f32[8,8,64,128]{3,2,1,0:T(8,128)}), f32[8,8,64,128]{3,2,1,0:T(8,128)S(1)}, u32[]{:S(2)}, u32[]{:S(2)}) %all-to-all-start.3) | async-done | bytes 2097184 | tf_op jit(solution)/shard_map/all_to_all | solution.py:23
  (60 shorter events, 16.9 us)
Async XLA Ops:
  0.6 13.3 %copy-start = (bf16[8,64,1024]{2,1,0:T(8,128)(2,1)S(1)}, bf16[8,64,1024]{2,1,0:T(8,128)(2,1)}, u32[]{:S(2)}) copy-start(bf16[8,64,1024]{2,1,0:T(8,128)(2,1)} %param.13) | copy-start | bytes 3145732
  0.6 14.0 %copy-start.3 = (f32[2,64,64]{2,1,0:T(8,128)S(1)}, f32[2,64,64]{2,1,0:T(8,128)}, u32[]{:S(2)}) copy-start(f32[2,64,64]{2,1,0:T(8,128)} %param.12) | copy-start | bytes 98308
  0.7 4.7 %collective-permute-start = (bf16[2,64,256]{2,1,0:T(8,128)(2,1)}, bf16[2,64,256]{2,1,0:T(8,128)(2,1)S(1)}, u32[]{:S(2)}, u32[]{:S(2)}) collective-permute-start(bf16[2,64,256]{2,1,0:T(8,128)(2,1)} %param.11), channel_id=1, source_target_pairs={{0,3},{1,0},{2,1},{3,2},{4,7},{5,4},{6,5},{7,6},{8,11},{9,8},{10,9... | collective-permute-start | bytes 196616 | tf_op jit(solution)/shard_map/ppermute | solution.py:13
  6.2 6.1 %collective-permute-start.1 = (bf16[2,64,512]{2,1,0:T(8,128)(2,1)S(1)}, bf16[2,64,512]{2,1,0:T(8,128)(2,1)S(1)}, u32[]{:S(2)}, u32[]{:S(2)}) collective-permute-start(bf16[2,64,512]{2,1,0:T(8,128)(2,1)S(1)} %pad_maximum_fusion), channel_id=1, source_target_pairs={{0,2},{1,3},{2,0},{3,1},{4,6},{5,7},{6,4},{7,5},{8,10},{9,11},{10,... | collective-permute-start | bytes 393224 | tf_op jit(solution)/shard_map/ppermute | solution.py:13
  13.2 0.8 copy-start.1
  17.0 3.8 %copy-start.4 = (s32[36,1]{0,1:T(1,128)S(1)}, s32[36,1]{0,1:T(1,128)}, u32[]{:S(2)}) copy-start(s32[36,1]{0,1:T(1,128)} %param.9) | copy-start | bytes 436
  86.7 29.2 %all-to-all-start.1 = ((f32[8,1,32768]{2,1,0:T(1,128)}), f32[8,1,32768]{2,1,0:T(1,128)S(1)}, u32[]{:S(2)}, u32[]{:S(2)}) async-start(f32[8,1,32768]{2,1,0:T(1,128)} %reshape.132), calls=%async_computation.1 | async-start | bytes 2097152 | tf_op jit(solution)/shard_map/all_to_all | solution.py:83
  117.4 65.1 %all-to-all-start.2 = ((f32[8,8,64,128]{3,2,1,0:T(8,128)}), f32[8,8,64,128]{3,2,1,0:T(8,128)}, u32[]{:S(2)}, u32[]{:S(2)}) async-start(f32[8,8,64,128]{3,2,1,0:T(8,128)} %broadcast_in_dim.12), calls=%async_computation.2 | async-start | bytes 4194304 | tf_op jit(solution)/shard_map/all_to_all | solution.py:30
  194.8 2.9 %copy-start.2 = (bf16[2,64,2048]{2,1,0:T(8,128)(2,1)S(1)}, bf16[2,64,2048]{2,1,0:T(8,128)(2,1)}, u32[]{:S(2)}) copy-start(bf16[2,64,2048]{2,1,0:T(8,128)(2,1)} %copy-done.1) | copy-start | bytes 1572868
  200.4 52.9 %all-to-all-start.3 = ((f32[8,8,64,128]{3,2,1,0:T(8,128)}), f32[8,8,64,128]{3,2,1,0:T(8,128)S(1)}, u32[]{:S(2)}, u32[]{:S(2)}) async-start(f32[8,8,64,128]{3,2,1,0:T(8,128)} %bitcast.113), calls=%async_computation.3 | async-start | bytes 4194304 | tf_op jit(solution)/shard_map/all_to_all | solution.py:23
